TPU v7x, 512 devices: a whole 4x8x8 slice. The times are simulated.
512 devices in a mesh: req: 128 (over z, y, core), head: 4 (over x).
Axes of the slice: x: 4, y: 8, z: 8, core: 2. Of those that a mesh axis runs over, the one named last changes fastest.
Arguments:
- hidden_in: bfloat16 [256, 2048], P(None, 'head'), may hold values from -1.5 to 1.5
- attention_gain: float32 [2048], replicated, may hold values from 0.1 to 1.9
- query_gain: float32 [64], replicated, may hold values from 0.5 to 2
- key_gain: float32 [64], replicated, may hold values from 1.5 to 4
- feedforward_gain: float32 [2048], replicated, may hold values from 0.1 to 1.9
- input_weight: bfloat16 [2048, 1920], P('req', 'head'), may hold values from -0.125 to 0.125
- output_weight: bfloat16 [1280, 2048], P('req', 'head'), may hold values from -0.15625 to 0.15625
- gate_weight: bfloat16 [2048, 5120], P('req', 'head'), may hold values from -0.125 to 0.125
- up_weight: bfloat16 [2048, 5120], P('req', 'head'), may hold values from -0.125 to 0.125
- down_weight: bfloat16 [5120, 2048], P('req', 'head'), may hold values from -0.078125 to 0.078125
- old_cache: bfloat16 [4096, 128, 640], P(('req', 'head')), may hold values from -400 to 400
- keep_rows: int32 [4096, 64], P(('req', 'head')), may hold values from -1 to 127, as said below
- drop_weights: float32 [4096, 128], P(('req', 'head')), may hold values from 0.1 to 1
- dest_slots: int32 [512, 8], P(('req', 'head')), may hold values from 0 to 7, each once within a row
- lengths: int32 [256], replicated, may hold values from 1 to 16, 2048 in all
- page_table: int32 [256, 16], P('req'), may hold values from 0 to 7, as said below
- source: int32 [128], replicated, may hold values from 0 to 127, each once
Outputs:
- compact_cache: bfloat16 [2048, 128, 640], P(('req', 'head'))
- summary_rows: bfloat16 [4096, 640], P(('req', 'head'))
- hidden_out: bfloat16 [256, 2048], P(None, 'head')
Inputs may be any that keep to these rules, and one draw needn't show every extreme that they name: `keep_rows`: row p lists kept rows of page p in ascending order, from 32 to 64 of them, then -1 to the end; some page keeps 64. `page_table`: row g * 2 + k belongs to the k-th request held by index g of req; entry j is the slot, on the device with req index g and head index j % 4, of that request's j-th page. On every device the entries that point to it form a permutation of its 8 slots. `source`: A permutation of the continued requests over the held slots. `dest_slots`: each row is a permutation. `lengths`: they sum to 2048 and the largest is 16.
All inputs are finite; a program needn't handle non-finite values.
Results may differ from a plain program's by a relative error of at most 0.015.
The roundings to bfloat16 on the way count: a program that leaves them out, or rounds other values in their place, can miss the bound.
Values may be sent and summed in bfloat16 or wider, within the bound.
A program may use at most 64 MiB of HBM per device.

v0:
```python
import jax
import jax.numpy as jnp
from jax import lax
from jax.sharding import PartitionSpec as P

D = 2048
HEADS = 20
KVH = 5
HD = 64
FF = 5120
PAGE = 128
KEEP = 64
NP = 16
R_DEV = 2
KVW = 640
epsilon = 1e-06
negative = -1e30


def joined(part, axis, combine):
    gathered = jax.tree.map(lambda a: lax.all_gather(a, axis), part)

    def take(source):
        return jax.tree.map(lambda a: lax.dynamic_index_in_dim(a, source, 0, False), gathered)

    return lax.fori_loop(
        1, lax.axis_size(axis), lambda source, state: combine(state, take(source)), take(0)
    )


def rms_rows(values, gain):
    mean_square = jnp.mean(values * values, axis=-1, keepdims=True)
    return values * lax.rsqrt(mean_square + epsilon) * gain


def rotate(vectors, positions):
    half = vectors.shape[-1] // 2
    frequency = 10000.0 ** (-jnp.arange(half, dtype=jnp.float32) / half)
    angles = positions.astype(jnp.float32)[:, None] * frequency[None, :]
    cosine = jnp.cos(angles)[:, None, :]
    sine = jnp.sin(angles)[:, None, :]
    first = vectors[..., :half]
    second = vectors[..., half:]
    return jnp.concatenate(
        [first * cosine - second * sine, second * cosine + first * sine], axis=-1
    )


def compact_pages(pages, keep, weights):
    rows = jnp.arange(pages.shape[1], dtype=jnp.int32)
    picks = keep[:, :, None] == rows[None, None, :]
    kept = jnp.einsum(
        "pkr,prc->pkc", picks.astype(jnp.bfloat16), pages, preferred_element_type=jnp.float32
    ).astype(jnp.bfloat16)
    dropped = weights * (1.0 - jnp.sum(picks.astype(jnp.float32), axis=1))
    total = jnp.sum(dropped, axis=1)
    means = (
        jnp.einsum(
            "pr,prc->pc", dropped, pages.astype(jnp.float32), precision=lax.Precision.HIGHEST
        )
        / total[:, None]
    )
    return (kept, means.astype(jnp.bfloat16), jnp.log(total))


def merge_parts(first, second):
    top_first, mass_first, sum_first = first
    top_second, mass_second, sum_second = second
    top = jnp.maximum(top_first, top_second)
    scale_first = jnp.exp(top_first - top)
    scale_second = jnp.exp(top_second - top)
    mass = mass_first * scale_first + mass_second * scale_second
    summed = sum_first * scale_first[..., None] + sum_second * scale_second[..., None]
    return (top, mass, summed)


def held_request(rows, source):
    half = R_DEV // 2
    position = rows % R_DEV
    slot = rows // R_DEV * half + position - half
    continued = jnp.arange(source.shape[0], dtype=jnp.int32)
    matches = source[None, :] == slot[:, None]
    owner_cont = jnp.sum(jnp.where(matches, continued[None, :], 0), axis=1)
    carried = owner_cont // half * R_DEV + half + owner_cont % half
    return jnp.where(position < half, rows, carried)


def full_rows(values):
    return lax.all_gather(values, "head", axis=1, tiled=True)


def feature_block(rows, count):
    return lax.dynamic_slice_in_dim(rows, lax.axis_index("req") * count, count, 1)


def normed_block(rows, gain, count):
    whole = full_rows(rows)
    normed = rms_rows(whole.astype(jnp.float32), gain).astype(jnp.bfloat16)
    return feature_block(normed, count)


def input_block(rows, count):
    return feature_block(full_rows(rows), count)


def project(inputs, weight):
    return lax.psum(jnp.dot(inputs, weight, preferred_element_type=jnp.float32), "req")


def on_device(
    hidden_in,
    attention_gain,
    query_gain,
    key_gain,
    feedforward_gain,
    input_weight,
    output_weight,
    gate_weight,
    up_weight,
    down_weight,
    old_cache,
    keep_rows,
    drop_weights,
    dest_slots,
    lengths,
    page_table,
    source,
):
    groups = lax.axis_size("req")
    lanes = lax.axis_size("head")
    group = lax.axis_index("req")
    lane = lax.axis_index("head")
    requests = hidden_in.shape[0]
    half = R_DEV // 2
    split = KVH * HD
    ratio = HEADS // KVH
    scale = HD ** (-0.5)
    pages_here = old_cache.shape[0]
    slots = jnp.arange(R_DEV, dtype=jnp.int32)
    held = held_request(group * R_DEV + slots, source)
    held_len = lengths[held]
    positions = held_len * PAGE
    inputs = normed_block(hidden_in, attention_gain, D // groups)
    partial_qkv = jnp.dot(inputs, input_weight, preferred_element_type=jnp.float32)
    mixed = lax.psum(partial_qkv, "req").astype(jnp.bfloat16)
    qkv = lax.all_gather(mixed, "head", axis=1, tiled=True)
    held_qkv = qkv[held].astype(jnp.float32)
    query = rotate(
        rms_rows(held_qkv[:, : HEADS * HD].reshape(R_DEV, HEADS, HD), query_gain), positions
    ).astype(jnp.bfloat16)
    key_new = rotate(
        rms_rows(held_qkv[:, HEADS * HD : (HEADS + KVH) * HD].reshape(R_DEV, KVH, HD), key_gain),
        positions,
    ).astype(jnp.bfloat16)
    value_new = held_qkv[:, (HEADS + KVH) * HD :].reshape(R_DEV, KVH, HD)
    kept, means, bias = compact_pages(old_cache, keep_rows, drop_weights)
    destination = dest_slots[0]
    fresh_ids = jnp.arange(pages_here, dtype=jnp.int32)
    inverse = jnp.sum(
        jnp.where(destination[None, :] == fresh_ids[:, None], fresh_ids[None, :], 0), axis=1
    )
    compact = kept[inverse].reshape(pages_here // 2, PAGE, KVW)
    summaries = means[inverse]
    per_lane = NP // lanes
    table = page_table.reshape(R_DEV, per_lane, lanes)
    mine = lax.dynamic_slice_in_dim(table, lane, 1, 2)[:, :, 0]
    logical = jnp.arange(per_lane, dtype=jnp.int32) * lanes + lane
    live = logical[None, :] < held_len[:, None]
    owner = jnp.any((mine[:, :, None] == fresh_ids[None, None, :]) & live[:, :, None], axis=1)
    query_groups = query.reshape(R_DEV, KVH, ratio, HD)
    row_keys = kept[:, :, :split].reshape(pages_here, KEEP, KVH, HD)
    row_values = kept[:, :, split:].reshape(pages_here, KEEP, KVH, HD)
    row_live = keep_rows >= 0
    allowed = owner[:, None, None, :, None] & row_live[None, None, None, :, :]
    scores = (
        jnp.einsum("rngd,pmnd->rngpm", query_groups, row_keys, preferred_element_type=jnp.float32)
        * scale
    )
    scores = jnp.where(allowed, scores, negative)
    mean_keys = means[:, :split].reshape(pages_here, KVH, HD)
    mean_values = means[:, split:].reshape(pages_here, KVH, HD)
    mean_scores = (
        jnp.einsum("rngd,pnd->rngp", query_groups, mean_keys, preferred_element_type=jnp.float32)
        * scale
        + bias[None, None, None, :]
    )
    mean_allowed = owner[:, None, None, :]
    mean_scores = jnp.where(mean_allowed, mean_scores, negative)
    top = jnp.maximum(jnp.max(scores, axis=(3, 4)), jnp.max(mean_scores, axis=3))
    row_weight = jnp.where(allowed, jnp.exp(scores - top[..., None, None]), 0.0)
    mean_weight = jnp.where(mean_allowed, jnp.exp(mean_scores - top[..., None]), 0.0)
    mass = jnp.sum(row_weight, axis=(3, 4)) + jnp.sum(mean_weight, axis=3)
    total = jnp.einsum(
        "rngpm,pmnd->rngd",
        row_weight,
        row_values.astype(jnp.float32),
        precision=lax.Precision.HIGHEST,
    )
    total = total + jnp.einsum(
        "rngp,pnd->rngd",
        mean_weight,
        mean_values.astype(jnp.float32),
        precision=lax.Precision.HIGHEST,
    )
    top, mass, total = joined((top, mass, total), "head", merge_parts)
    own_score = (
        jnp.einsum("rngd,rnd->rng", query_groups, key_new, preferred_element_type=jnp.float32)
        * scale
    )
    final_top = jnp.maximum(top, own_score)
    earlier = jnp.exp(top - final_top)
    own_weight = jnp.exp(own_score - final_top)
    mass = mass * earlier + own_weight
    total = total * earlier[..., None] + own_weight[..., None] * value_new[:, :, None, :]
    attention = (total / mass[..., None]).reshape(R_DEV, HEADS * HD).astype(jnp.bfloat16)
    moved = lax.all_to_all(attention, "req", split_axis=1, concat_axis=0, tiled=True)
    everyone = jnp.arange(requests, dtype=jnp.int32)
    position = everyone % R_DEV
    cont_index = everyone // R_DEV * half + position - half
    slot_of = source[jnp.clip(cont_index, 0, source.shape[0] - 1)]
    held_row = slot_of // half * R_DEV + half + slot_of % half
    row_of = jnp.where(position < half, everyone, held_row)
    attention_rows = moved[row_of]
    projected = project(attention_rows, output_weight)
    mid = (hidden_in.astype(jnp.float32) + projected).astype(jnp.bfloat16)
    inputs_mid = normed_block(mid, feedforward_gain, D // groups)
    both = jnp.concatenate([gate_weight, up_weight], axis=1)
    local_units = gate_weight.shape[1]
    sums = lax.psum(jnp.dot(inputs_mid, both, preferred_element_type=jnp.float32), "req")
    active = (jax.nn.silu(sums[:, :local_units]) * sums[:, local_units:]).astype(jnp.bfloat16)
    down = project(input_block(active, FF // groups), down_weight)
    residual = lax.optimization_barrier(mid).astype(jnp.float32)
    result = (residual + down).astype(jnp.bfloat16)
    return (compact, summaries, result)


def solution(mesh):
    placed = (
        P(None, "head"),
        P(),
        P(),
        P(),
        P(),
        P("req", "head"),
        P("req", "head"),
        P("req", "head"),
        P("req", "head"),
        P("req", "head"),
        P(("req", "head"), None, None),
        P(("req", "head"), None),
        P(("req", "head"), None),
        P(("req", "head"), None),
        P(),
        P("req", None),
        P(),
    )
    return jax.shard_map(
        on_device,
        mesh=mesh,
        in_specs=placed,
        out_specs=(P(("req", "head"), None, None), P(("req", "head"), None), P(None, "head")),
        check_vma=False,
    )
```

profile of v0, /device:TPU:24, one launch (start us, length us, event | category | flops | bytes accessed | tf_op | source)
XLA Modules:
  0.0 1286.6 jit_solution(14385195051736186096)
XLA Ops:
  7.2 0.7 all-gather.7.cloned.1.call-update
  8.0 0.8 fusion.49
  8.8 1.9 gather_fusion.4
  10.7 0.8 reshape.428
  11.5 1.3 gather_fusion.2
  13.3 0.8 convert_reduce_fusion
  14.2 0.8 fusion.64
  15.0 1.1 convolution_convert_fusion
  16.1 0.7 fusion.70
  17.3 1.1 copy.94
  18.5 1.1 copy.84
  19.6 0.8 dynamic-slice
  20.6 23.2 %all-gather.7.cloned.1.call-done = bf16[256,2048]{1,0:T(8,128)(2,1)} async-done(((bf16[256,512]{1,0:T(8,128)(2,1)}), bf16[256,2048]{1,0:T(8,128)(2,1)}) %all-gather.7.cloned.1.call-update) | async-done | bytes 1048592 | tf_op jit(solution)/shard_map/all_gather | solution.py:89
  43.8 1.5 multiply_reduce_fusion.1
  45.3 1.5 convert_element_type.68
  46.8 0.4 fusion.23
  47.2 480.6 %all-reduce.10 = bf16[256,480]{0,1:T(8,128)(2,1)S(1)} all-reduce(f32[256,480]{0,1:T(8,128)S(1)} %fusion.23), channel_id=1, replica_groups=mesh['req'=128,'head'=4] {'req'}, use_global_device_ids=true, to_apply=%region_6.7 | all-reduce | flops 122880 | bytes 737280 | tf_op jit(solution)/shard_map/psum | solution.py:145
  527.8 14.1 %all_gather.27 = bf16[256,1920]{0,1:T(8,128)(2,1)S(1)} all-gather(bf16[256,480]{0,1:T(8,128)(2,1)S(1)} %all-reduce.10), channel_id=1, replica_groups=mesh['req'=128,'head'=4] {'head'}, dimensions={1}, use_global_device_ids=true | all-gather | bytes 1228800 | tf_op jit(solution)/shard_map/all_gather | solution.py:146
  542.0 1.4 copy.85
  543.4 2.0 gather_fusion.3
  546.6 1.4 fusion.68
  548.3 0.2 fusion.63
  548.9 11.9 all-gather.1
  560.8 11.9 all-gather
  572.7 0.6 convolution_bitcast_fusion
  573.3 0.2 fusion.7
  573.6 11.9 all-gather.2
  585.5 1.1 while.19
  587.1 0.7 copy.103
  587.8 21.1 %all-to-all-start = ((bf16[2,128,10]{2,0,1:T(2,128)(2,1)}), bf16[2,128,10]{2,0,1:T(2,128)(2,1)S(1)}, u32[]{:S(2)}, u32[]{:S(2)}) async-start(bf16[2,128,10]{2,0,1:T(2,128)(2,1)} %copy.103), calls=%async_computation | async-start | bytes 131072 | tf_op jit(solution)/shard_map/all_to_all | solution.py:216
  609.0 9.2 all-to-all-done
  618.2 0.9 gather_fusion.5
  619.1 1.0 fusion.71
  620.2 185.8 %all-reduce.5.cloned.1.call-done = f32[256,512]{1,0:T(8,128)} async-done(((f32[256,512]{1,0:T(8,128)}), f32[256,512]{1,0:T(8,128)}) %all-reduce.5.cloned.1.call-update) | async-done | bytes 524304 | tf_op jit(solution)/shard_map/psum | solution.py:107
  805.9 1.8 add_convert_fusion.1
  807.8 0.8 dynamic-slice.1
  808.6 25.2 %all-gather.9.cloned.1.call-done = bf16[256,2048]{1,0:T(8,128)(2,1)} async-done(((bf16[256,512]{1,0:T(8,128)(2,1)}), bf16[256,2048]{1,0:T(8,128)(2,1)}) %all-gather.9.cloned.1.call-update) | async-done | bytes 1048592 | tf_op jit(solution)/shard_map/all_gather | solution.py:89
  833.8 1.5 multiply_reduce_fusion
  835.4 1.5 convert_element_type.77
  836.8 2.1 fusion.19
  839.0 203.2 %all-reduce.7.cloned.1.call-done = f32[256,2560]{1,0:T(8,128)} async-done(((f32[256,2560]{1,0:T(8,128)}), f32[256,2560]{1,0:T(8,128)}) %all-reduce.7.cloned.1.call-update) | async-done | bytes 2621456 | tf_op jit(solution)/shard_map/psum | solution.py:229
  1042.2 2.9 fusion.4
  1045.3 36.2 %all-gather.11.cloned.1.call-done = bf16[256,5120]{1,0:T(8,128)(2,1)} async-done(((bf16[256,1280]{1,0:T(8,128)(2,1)}), bf16[256,5120]{1,0:T(8,128)(2,1)}) %all-gather.11.cloned.1.call-update) | async-done | bytes 2621456 | tf_op jit(solution)/shard_map/all_gather | solution.py:89
  1081.6 2.0 fusion.30
  1083.6 1.2 gather_fusion.1
  1084.8 1.5 gather_fusion
  1086.3 191.7 %all-reduce.9.cloned.1.call-done = f32[256,512]{1,0:T(8,128)} async-done(((f32[256,512]{1,0:T(8,128)}), f32[256,512]{1,0:T(8,128)}) %all-reduce.9.cloned.1.call-update) | async-done | bytes 524304 | tf_op jit(solution)/shard_map/psum | solution.py:107
  1278.0 1.8 add_convert_fusion
  (115 shorter events, 5.3 us)
Async XLA Ops:
  7.2 7.8 copy-start
  7.2 36.6 %all-gather.7.cloned.1.call-start = ((), (), s32[]{:S(2)}) async-start(), calls=%async_computation.1 | async-start | bytes 1310720 | tf_op jit(solution)/shard_map/all_gather | solution.py:89
  16.8 3.7 copy-start.7
  20.6 26.2 %copy-start.8 = (bf16[16,480]{1,0:T(8,128)(2,1)S(1)}, bf16[16,480]{1,0:T(8,128)(2,1)}, u32[]{:S(2)}) copy-start(bf16[16,480]{1,0:T(8,128)(2,1)} %param.24) | copy-start | bytes 46084
  47.2 498.6 %copy-start.11 = (f32[64]{0:T(128)S(1)}, f32[64]{0:T(128)}, u32[]{:S(2)}) copy-start(f32[64]{0:T(128)} %param.22) | copy-start | bytes 772
  47.2 498.7 %copy-start.10 = (f32[64]{0:T(128)S(1)}, f32[64]{0:T(128)}, u32[]{:S(2)}) copy-start(f32[64]{0:T(128)} %param.21) | copy-start | bytes 772
  543.4 29.3 %copy-start.3 = (bf16[8,64,320]{1,2,0:T(8,128)(2,1)S(1)}, bf16[8,64,320]{1,2,0:T(8,128)(2,1)}, u32[]{:S(2)}) copy-start(bf16[8,64,320]{1,2,0:T(8,128)(2,1)} %copy.94) | copy-start | bytes 983044
  548.0 71.1 %copy-start.9 = (bf16[10,512]{1,0:T(8,128)(2,1)S(1)}, bf16[10,512]{1,0:T(8,128)(2,1)}, u32[]{:S(2)}) copy-start(bf16[10,512]{1,0:T(8,128)(2,1)} %param.25) | copy-start | bytes 30724
  572.7 233.2 %copy-start.2 = (bf16[256,512]{1,0:T(8,128)(2,1)S(1)}, bf16[256,512]{1,0:T(8,128)(2,1)}, u32[]{:S(2)}) copy-start(bf16[256,512]{1,0:T(8,128)(2,1)} %param.19) | copy-start | bytes 786436
  587.8 30.4 %all-to-all-start = ((bf16[2,128,10]{2,0,1:T(2,128)(2,1)}), bf16[2,128,10]{2,0,1:T(2,128)(2,1)S(1)}, u32[]{:S(2)}, u32[]{:S(2)}) async-start(bf16[2,128,10]{2,0,1:T(2,128)(2,1)} %copy.103), calls=%async_computation | async-start | bytes 131072 | tf_op jit(solution)/shard_map/all_to_all | solution.py:216
  608.9 197.0 %all-reduce.5.cloned.1.call-start = ((), (), s32[]{:S(2)}) async-start(), calls=%async_computation.2 | async-start | bytes 1048576 | tf_op jit(solution)/shard_map/psum | solution.py:107
  620.1 213.7 %all-gather.9.cloned.1.call-start = ((), (), s32[]{:S(2)}) async-start(), calls=%async_computation.3 | async-start | bytes 1310720 | tf_op jit(solution)/shard_map/all_gather | solution.py:89
  807.8 234.5 %all-reduce.7.cloned.1.call-start = ((), (), s32[]{:S(2)}) async-start(), calls=%async_computation.4 | async-start | bytes 5242880 | tf_op jit(solution)/shard_map/psum | solution.py:229
  808.6 28.2 %copy-start.5 = (bf16[16,1280]{1,0:T(8,128)(2,1)S(1)}, bf16[16,1280]{1,0:T(8,128)(2,1)}, u32[]{:S(2)}) copy-start(bf16[16,1280]{1,0:T(8,128)(2,1)} %param.27) | copy-start | bytes 122884
  808.6 28.2 %copy-start.6 = (bf16[16,1280]{1,0:T(8,128)(2,1)S(1)}, bf16[16,1280]{1,0:T(8,128)(2,1)}, u32[]{:S(2)}) copy-start(bf16[16,1280]{1,0:T(8,128)(2,1)} %param.26) | copy-start | bytes 122884
  839.0 206.3 %copy-start.12 = (s32[1,8]{1,0:T(1,128)S(1)}, s32[1,8]{1,0:T(1,128)}, u32[]{:S(2)}) copy-start(s32[1,8]{1,0:T(1,128)} %param.32) | copy-start | bytes 100
  839.0 242.6 %copy-start.4 = (bf16[40,512]{1,0:T(8,128)(2,1)S(1)}, bf16[40,512]{1,0:T(8,128)(2,1)}, u32[]{:S(2)}) copy-start(bf16[40,512]{1,0:T(8,128)(2,1)} %param.28) | copy-start | bytes 122884
  839.0 242.6 %all-gather.11.cloned.1.call-start = ((), (), s32[]{:S(2)}) async-start(), calls=%async_computation.5 | async-start | bytes 3276800 | tf_op jit(solution)/shard_map/all_gather | solution.py:89
  1045.1 232.8 %copy-start.1 = (bf16[256,512]{1,0:T(8,128)(2,1)S(1)}, bf16[256,512]{1,0:T(8,128)(2,1)}, u32[]{:S(2)}) copy-start(bf16[256,512]{1,0:T(8,128)(2,1)} %add_convert_fusion.1) | copy-start | bytes 786436
  1045.2 232.8 %all-reduce.9.cloned.1.call-start = ((), (), s32[]{:S(2)}) async-start(), calls=%async_computation.6 | async-start | bytes 1048576 | tf_op jit(solution)/shard_map/psum | solution.py:107
Sparse Core Ops, SparseCore 0:
  10.1 33.6 all-gather.6
  620.2 185.6 all-reduce.4
  808.6 25.1 all-gather.8
  839.1 203.0 all-reduce.6
  1045.3 36.2 all-gather.10
  1085.0 192.9 all-reduce.8
where the time goes:
time: 1290 us
  waiting for transfers between devices  675 us (52%)
  blocking collectives  530 us (41%)
  starting transfers between devices  21.3 us (2%)
  local copies, waits for them, and re-layouts  17.8 us (1%)
  other arithmetic  17.2 us (1%)
  between operations  14.5 us (1%)
    psum x1, blocking collectives, on_device(): mixed = lax.psum(partial_qkv, 'req').astype(jnp.bfloat16)  481 us
    psum x2, waiting for transfers between devices, project(): lax.psum(jnp.dot(inputs, weight, preferred_element_type=jnp.float32), 'req')  378 us
    psum x1, waiting for transfers between devices, on_device(): lax.psum(jnp.dot(inputs_mid, both, preferred_element_type=jnp.float32), '...  203 us
    all_gather x3, waiting for transfers between devices, full_rows(): return lax.all_gather(values, 'head', axis=1, tiled=True)  84.7 us
    all_gather x3, blocking collectives, joined(): gathered = jax.tree.map(lambda a: lax.all_gather(a, axis), part)  35.7 us
  transfers between devices with their start and end apart: 7, of which 7 were waited for; matrix products, arithmetic and copies ran while one was open for 1% of the time, Pallas kernels for 0%

commit v1 on v0

--- a/solution.py
+++ b/solution.py
@@ -15,6 +15,27 @@
 KVW = 640
 epsilon = 1e-06
 negative = -1e30
+
+
+def ring_gather(x, axis, dim):
+    peers, index, width = (lax.axis_size(axis), lax.axis_index(axis), x.shape[dim])
+    upward = [(i, (i + 1) % peers) for i in range(peers)]
+    behind = [(i, (i - 1) % peers) for i in range(peers)]
+    out = jnp.zeros((*x.shape[:dim], peers * width, *x.shape[dim + 1 :]), x.dtype)
+    out = lax.dynamic_update_slice_in_dim(out, x, index * width, axis=dim)
+    from_left = from_right = x
+    half = peers // 2
+    for step in range(1, half + 1):
+        from_left = lax.ppermute(from_left, axis, upward)
+        out = lax.dynamic_update_slice_in_dim(
+            out, from_left, (index - step) % peers * width, axis=dim
+        )
+        if step < peers - half:
+            from_right = lax.ppermute(from_right, axis, behind)
+            out = lax.dynamic_update_slice_in_dim(
+                out, from_right, (index + step) % peers * width, axis=dim
+            )
+    return out
 
 
 def joined(part, axis, combine):
@@ -86,7 +107,7 @@
 
 
 def full_rows(values):
-    return lax.all_gather(values, "head", axis=1, tiled=True)
+    return ring_gather(values, "head", 1)
 
 
 def feature_block(rows, count):

time: 1290 us -> 1270 us (0.984)
  waiting for transfers between devices: 675 us -> 614 us
  starting transfers between devices: 21.3 us -> 49 us
  local copies, waits for them, and re-layouts: 17.8 us -> 31.8 us
    all_gather x3 -> x0, waiting for transfers between devices: 84.7 us -> none  [full_rows(): return lax.all_gather(values, 'head', axis=1, tiled=True)]
    ppermute x0 -> x9, waiting for transfers between devices: none -> 34.5 us  [the longest x6 34.5 us: ring_gather(): from_left = lax.ppermute(from_left, axis, upward)]
    ppermute x0 -> x9, starting transfers between devices: none -> 27.8 us  [the longest x6 15.7 us: ring_gather(): from_left = lax.ppermute(from_left, axis, upward)]
  transfers between devices with their start and end apart: 7 -> 13, of which waited for: 7 -> 9; matrix products, arithmetic and copies ran while one was open for 1% -> 2% of each run, Pallas kernels for 0% -> 0%
where the time goes in v1:
time: 1270 us
  waiting for transfers between devices  614 us (48%)
  blocking collectives  536 us (42%)
  starting transfers between devices  49 us (4%)
  local copies, waits for them, and re-layouts  31.8 us (3%)
  between operations  14.4 us (1%)
    psum x1, blocking collectives, on_device(): mixed = lax.psum(partial_qkv, 'req').astype(jnp.bfloat16)  486 us
    psum x2, waiting for transfers between devices, project(): lax.psum(jnp.dot(inputs, weight, preferred_element_type=jnp.float32), 'req')  372 us
    psum x1, waiting for transfers between devices, on_device(): lax.psum(jnp.dot(inputs_mid, both, preferred_element_type=jnp.float32), '...  199 us
    all_gather x3, blocking collectives, joined(): gathered = jax.tree.map(lambda a: lax.all_gather(a, axis), part)  35.7 us
    ppermute x6, waiting for transfers between devices, ring_gather(): from_left = lax.ppermute(from_left, axis, upward)  34.5 us
  transfers between devices with their start and end apart: 13, of which 9 were waited for; matrix products, arithmetic and copies ran while one was open for 2% of the time, Pallas kernels for 0%

profile of v1, /device:TPU:24, one launch (start us, length us, event | category | flops | bytes accessed | tf_op | source)
XLA Modules:
  0.0 1265.9 jit_solution(17888050639050232173)
XLA Ops:
  7.2 4.8 collective-permute-start.1
  12.0 1.9 collective-permute-start
  16.4 1.9 gather_fusion.4
  18.3 1.3 gather_fusion.2
  20.9 1.1 convolution_convert_fusion
  23.0 1.0 fusion.66
  24.2 2.7 collective-permute-start.2
  27.0 1.0 constant_dynamic-update-slice_fusion.11
  28.2 2.1 copy.94
  30.3 1.1 copy.84
  33.2 1.0 constant_dynamic-update-slice_fusion.9
  34.1 1.2 collective-permute-done.2
  35.4 1.0 constant_dynamic-update-slice_fusion.8
  37.5 485.8 %all-reduce.10 = bf16[256,480]{0,1:T(8,128)(2,1)S(1)} all-reduce(f32[256,480]{0,1:T(8,128)S(1)} %fusion.23), channel_id=1, replica_groups=mesh['req'=128,'head'=4] {'req'}, use_global_device_ids=true, to_apply=%region_6.7 | all-reduce | flops 122880 | bytes 737280 | tf_op jit(solution)/shard_map/psum | solution.py:166
  523.2 14.5 %all_gather.17 = bf16[256,1920]{0,1:T(8,128)(2,1)S(1)} all-gather(bf16[256,480]{0,1:T(8,128)(2,1)S(1)} %all-reduce.10), channel_id=1, replica_groups=mesh['req'=128,'head'=4] {'head'}, dimensions={1}, use_global_device_ids=true | all-gather | bytes 1228800 | tf_op jit(solution)/shard_map/all_gather | solution.py:167
  537.8 1.4 copy.85
  539.2 2.0 gather_fusion.3
  542.5 1.4 fusion.69
  544.7 11.9 all-gather.1
  556.6 11.9 all-gather
  569.4 11.9 all-gather.2
  581.3 1.1 while.19
  583.7 21.0 %all-to-all-start = ((bf16[2,128,10]{2,0,1:T(2,128)(2,1)}), bf16[2,128,10]{2,0,1:T(2,128)(2,1)S(1)}, u32[]{:S(2)}, u32[]{:S(2)}) async-start(bf16[2,128,10]{2,0,1:T(2,128)(2,1)} %copy.103), calls=%async_computation | async-start | bytes 131072 | tf_op jit(solution)/shard_map/all_to_all | solution.py:237
  604.8 9.2 all-to-all-done
  614.9 1.0 fusion.72
  615.9 185.7 %all-reduce.5.cloned.1.call-done = f32[256,512]{1,0:T(8,128)} async-done(((f32[256,512]{1,0:T(8,128)}), f32[256,512]{1,0:T(8,128)}) %all-reduce.5.cloned.1.call-update) | async-done | bytes 524304 | tf_op jit(solution)/shard_map/psum | solution.py:128
  801.7 1.1 constant_dynamic-update-slice_fusion.7
  802.9 3.4 collective-permute-start.3
  806.2 3.7 collective-permute-start.4
  809.9 3.4 collective-permute-done.3
  813.3 2.2 collective-permute-start.5
  816.3 6.5 collective-permute-done.5
  823.6 2.1 fusion.19
  825.8 198.6 %all-reduce.7.cloned.1.call-done = f32[256,2560]{1,0:T(8,128)} async-done(((f32[256,2560]{1,0:T(8,128)}), f32[256,2560]{1,0:T(8,128)}) %all-reduce.7.cloned.1.call-update) | async-done | bytes 2621456 | tf_op jit(solution)/shard_map/psum | solution.py:250
  1024.4 1.8 broadcast_in_dim.78
  1027.1 1.3 constant_dynamic-update-slice_fusion.3
  1028.4 3.4 collective-permute-start.6
  1031.7 3.7 collective-permute-start.7
  1035.4 11.5 collective-permute-done.6
  1046.9 2.2 collective-permute-start.8
  1050.7 2.0 constant_dynamic-update-slice_fusion.1
  1052.7 11.9 collective-permute-done.8
  1064.6 2.0 constant_dynamic-update-slice_fusion
  1066.6 2.0 fusion.30
  1068.6 1.2 gather_fusion.1
  1069.8 1.5 gather_fusion
  1071.3 186.3 %all-reduce.9.cloned.1.call-done = f32[256,512]{1,0:T(8,128)} async-done(((f32[256,512]{1,0:T(8,128)}), f32[256,512]{1,0:T(8,128)}) %all-reduce.9.cloned.1.call-update) | async-done | bytes 524304 | tf_op jit(solution)/shard_map/psum | solution.py:128
  1257.6 1.8 add_convert_fusion
  (139 shorter events, 18.4 us)
Async XLA Ops:
  7.2 13.7 %copy-start = (bf16[8,128,640]{2,1,0:T(8,128)(2,1)S(1)}, bf16[8,128,640]{2,1,0:T(8,128)(2,1)}, u32[]{:S(2)}) copy-start(bf16[8,128,640]{2,1,0:T(8,128)(2,1)} %param.29) | copy-start | bytes 3932164
  7.2 14.8 %copy-start.9 = (f32[8,128]{1,0:T(8,128)S(1)}, f32[8,128]{1,0:T(8,128)}, u32[]{:S(2)}) copy-start(f32[8,128]{1,0:T(8,128)} %param.31) | copy-start | bytes 12292
  7.2 26.0 %collective-permute-start.1 = (bf16[256,512]{1,0:T(8,128)(2,1)}, bf16[256,512]{1,0:T(8,128)(2,1)}, u32[]{:S(2)}, u32[]{:S(2)}) collective-permute-start(bf16[256,512]{1,0:T(8,128)(2,1)} %param.19), channel_id=1, source_target_pairs={{0,3},{1,0},{2,1},{3,2},{4,7},{5,4},{6,5},{7,6},{8,11},{9,8},{10,9... | collective-permute-start | bytes 786440 | tf_op jit(solution)/shard_map/ppermute | solution.py:34
  12.0 12.2 collective-permute-start
  24.2 11.2 collective-permute-start.2
  36.3 0.7 copy-start.7
  37.5 504.2 %copy-start.11 = (f32[64]{0:T(128)S(1)}, f32[64]{0:T(128)}, u32[]{:S(2)}) copy-start(f32[64]{0:T(128)} %param.22) | copy-start | bytes 772
  37.5 504.3 %copy-start.10 = (f32[64]{0:T(128)S(1)}, f32[64]{0:T(128)}, u32[]{:S(2)}) copy-start(f32[64]{0:T(128)} %param.21) | copy-start | bytes 772
  539.2 29.3 %copy-start.3 = (bf16[8,64,320]{1,2,0:T(8,128)(2,1)S(1)}, bf16[8,64,320]{1,2,0:T(8,128)(2,1)}, u32[]{:S(2)}) copy-start(bf16[8,64,320]{1,2,0:T(8,128)(2,1)} %copy.94) | copy-start | bytes 983044
  543.8 71.0 %copy-start.8 = (bf16[10,512]{1,0:T(8,128)(2,1)S(1)}, bf16[10,512]{1,0:T(8,128)(2,1)}, u32[]{:S(2)}) copy-start(bf16[10,512]{1,0:T(8,128)(2,1)} %param.25) | copy-start | bytes 30724
  581.3 220.4 %copy-start.2 = (bf16[256,512]{1,0:T(8,128)(2,1)S(1)}, bf16[256,512]{1,0:T(8,128)(2,1)}, u32[]{:S(2)}) copy-start(bf16[256,512]{1,0:T(8,128)(2,1)} %param.19) | copy-start | bytes 786436
  583.7 30.3 %all-to-all-start = ((bf16[2,128,10]{2,0,1:T(2,128)(2,1)}), bf16[2,128,10]{2,0,1:T(2,128)(2,1)S(1)}, u32[]{:S(2)}, u32[]{:S(2)}) async-start(bf16[2,128,10]{2,0,1:T(2,128)(2,1)} %copy.103), calls=%async_computation | async-start | bytes 131072 | tf_op jit(solution)/shard_map/all_to_all | solution.py:237
  604.7 196.9 %all-reduce.5.cloned.1.call-start = ((), (), s32[]{:S(2)}) async-start(), calls=%async_computation.1 | async-start | bytes 1048576 | tf_op jit(solution)/shard_map/psum | solution.py:128
  615.9 408.5 %all-reduce.7.cloned.1.call-start = ((), (), s32[]{:S(2)}) async-start(), calls=%async_computation.2 | async-start | bytes 5242880 | tf_op jit(solution)/shard_map/psum | solution.py:250
  802.9 10.4 collective-permute-start.3
  806.2 10.0 collective-permute-start.4
  813.3 9.5 collective-permute-start.5
  822.8 0.8 copy-start.5
  822.8 0.8 copy-start.6
  825.7 431.8 %all-reduce.9.cloned.1.call-start = ((), (), s32[]{:S(2)}) async-start(), calls=%async_computation.3 | async-start | bytes 1048576 | tf_op jit(solution)/shard_map/psum | solution.py:128
  1024.4 2.7 copy-start.1
  1027.1 22.0 %copy-start.12 = (s32[1,8]{1,0:T(1,128)S(1)}, s32[1,8]{1,0:T(1,128)}, u32[]{:S(2)}) copy-start(s32[1,8]{1,0:T(1,128)} %param.32) | copy-start | bytes 100
  1028.4 18.5 %collective-permute-start.6 = (bf16[256,1280]{1,0:T(8,128)(2,1)S(1)}, bf16[256,1280]{1,0:T(8,128)(2,1)S(1)}, u32[]{:S(2)}, u32[]{:S(2)}) collective-permute-start(bf16[256,1280]{1,0:T(8,128)(2,1)S(1)} %get-tuple-element.231), channel_id=1, source_target_pairs={{0,1},{1,2},{2,3},{3,0},{4,5},{5,6},{6,7},{7,4},{8,9},{9,10},{10,1... | collective-permute-start | bytes 1966088 | tf_op jit(solution)/shard_map/ppermute | solution.py:29
  1031.7 18.9 %collective-permute-start.7 = (bf16[256,1280]{1,0:T(8,128)(2,1)S(1)}, bf16[256,1280]{1,0:T(8,128)(2,1)}, u32[]{:S(2)}, u32[]{:S(2)}) collective-permute-start(bf16[256,1280]{1,0:T(8,128)(2,1)S(1)} %get-tuple-element.231), channel_id=1, source_target_pairs={{0,3},{1,0},{2,1},{3,2},{4,7},{5,4},{6,5},{7,6},{8,11},{9,8},{10,9... | collective-permute-start | bytes 1966088 | tf_op jit(solution)/shard_map/ppermute | solution.py:34
  1046.9 17.7 %collective-permute-start.8 = (bf16[256,1280]{1,0:T(8,128)(2,1)S(1)}, bf16[256,1280]{1,0:T(8,128)(2,1)}, u32[]{:S(2)}, u32[]{:S(2)}) collective-permute-start(bf16[256,1280]{1,0:T(8,128)(2,1)S(1)} %collective-permute-done.6), channel_id=1, source_target_pairs={{0,1},{1,2},{2,3},{3,0},{4,5},{5,6},{6,7},{7,4},{8,9},{9,10},{10,1... | collective-permute-start | bytes 1966088 | tf_op jit(solution)/shard_map/ppermute | solution.py:29
  1049.1 17.5 %copy-start.4 = (bf16[40,512]{1,0:T(8,128)(2,1)S(1)}, bf16[40,512]{1,0:T(8,128)(2,1)}, u32[]{:S(2)}) copy-start(bf16[40,512]{1,0:T(8,128)(2,1)} %param.28) | copy-start | bytes 122884
  1050.7 17.9 %copy-start.13 = (s32[8]{0:T(128)S(1)}, s32[8]{0:T(128)}, u32[]{:S(2)}) copy-start(s32[8]{0:T(128)} %select_reduce_fusion) | copy-start | bytes 100
Sparse Core Ops, SparseCore 0:
  616.0 185.5 all-reduce.4
  825.9 198.4 all-reduce.6
  1068.7 188.8 all-reduce.8
